TPU v7x, 32 devices: a whole 2x2x4 slice. The times are simulated.
32 devices in a mesh: grp: 2 (over z_hi), seq: 8 (over y, x, core), tp: 2 (over z_lo).
Axes of the slice: x: 2, y: 2, z: 4 (z_hi: 2, z_lo: 2; z = z_hi * 2 + z_lo), core: 2. Of those that a mesh axis runs over, the one named last changes fastest.
Arguments:
- latents: bfloat16 [2, 64, 2048], P('grp', None, 'seq'), may hold values from -6 to 6
- patch_weight: bfloat16 [128, 5120], replicated, may hold values from -0.5 to 0.5
- patch_bias: float32 [5120], replicated, may hold values from -3 to 3
- modulation: float32 [3, 5120], replicated, may hold values from -3 to 3
- qkv_weight: bfloat16 [5120, 3, 1024], P(None, None, 'seq'), may hold values from -0.078125 to 0.078125
- norm_gain: float32 [2, 1024], P(None, 'seq'), may hold values from 0.5 to 16
- out_weight: bfloat16 [1024, 5120], P('seq', ('grp', 'tp')), may hold values from -0.5 to 0.5
- token_order: int32 [2048], replicated, may hold values from 0 to 2047, each once
- window_start: int32 [1], replicated, may hold values from 0 to 1024
Outputs:
- attended: bfloat16 [1024, 5120], P('seq', ('grp', 'tp'))
Inputs may be any that keep to these rules, and one draw needn't show every extreme that they name: Position j of the target layout holds frame-major token token_order[j]; every token stands once. The window covers target positions window_start[0] to window_start[0] + 1023.
All inputs are finite; a program needn't handle non-finite values.
Results may differ from a plain program's by a relative error of at most 0.018.
The roundings to bfloat16 on the way count: a program that leaves them out, or rounds other values in their place, can miss the bound.
Values may be sent and summed in bfloat16 or wider, within the bound.
A program may use at most 128 MiB of HBM per device.

v0:
```python
import math
import jax
import jax.numpy as jnp
from jax import lax
from jax.sharding import PartitionSpec as P

QW_DEV = 128
norm_eps = 0.1


def swapped(block, axis, apart):
    count = lax.axis_size(axis)
    route = []
    for low in range(count):
        high = low | 1 << apart
        if high != low and high < count:
            route += [(low, high), (high, low)]
    return lax.ppermute(block, axis, route)


def joined(array, axis, combine):
    everything = jax.tree.map(lambda part: lax.all_gather(part, axis), array)
    initial = jax.tree.map(lambda part: part[0], everything)

    def step(k, so_far):
        return combine(so_far, jax.tree.map(lambda part: part[k], everything))

    return lax.fori_loop(1, lax.axis_size(axis), step, initial)


def embed_rows(columns, patch_weight, patch_bias, modulation):
    channels = columns.shape[1]
    weight = patch_weight.reshape(2, channels, patch_weight.shape[1])
    embedded = (
        lax.dot_general(
            columns, weight, (((0, 1), (0, 1)), ((), ())), preferred_element_type=jnp.float32
        )
        + patch_bias
    )
    centre = embedded - jnp.mean(embedded, axis=1, keepdims=True)
    spread = jnp.mean(centre * centre, axis=1, keepdims=True)
    normed = centre * lax.rsqrt(spread + norm_eps) * (1.0 + modulation[1]) + modulation[0]
    return normed.astype(jnp.bfloat16)


def project_rows(columns, flat_weight, patch_weight, patch_bias, modulation):
    row_total = columns.shape[2]
    block = math.gcd(row_total, 512)

    def one_block(block_index):
        section = lax.dynamic_slice_in_dim(columns, block_index * block, block, 2)
        normed = embed_rows(section, patch_weight, patch_bias, modulation)
        return jnp.dot(normed, flat_weight, preferred_element_type=jnp.float32)

    result = lax.map(one_block, jnp.arange(row_total // block))
    return result.reshape(row_total, flat_weight.shape[1])


def per_device(
    latents,
    patch_weight,
    patch_bias,
    modulation,
    qkv_weight,
    norm_gain,
    out_weight,
    token_order,
    window_start,
):
    head_dim = qkv_weight.shape[2]
    seq_count = lax.axis_size("seq")
    groups = lax.axis_size("grp") * lax.axis_size("tp")
    quarter = lax.axis_index("grp") * lax.axis_size("tp") + lax.axis_index("tp")
    partner = swapped(latents, "grp", 0)
    is_high = lax.axis_index("grp") == 0
    paired = jnp.where(
        is_high, jnp.concatenate([latents, partner], 0), jnp.concatenate([partner, latents], 0)
    )
    gathered = lax.all_gather(paired, "seq", axis=2, tiled=True)
    tokens = gathered.shape[2]
    key_count = tokens // groups
    flat_weight = qkv_weight.reshape(qkv_weight.shape[0], 3 * head_dim)
    key_columns = lax.dynamic_slice_in_dim(gathered, quarter * key_count, key_count, 2)
    pair_raw = project_rows(
        key_columns, flat_weight[:, head_dim:], patch_weight, patch_bias, modulation
    )
    key_raw = pair_raw[:, :head_dim]
    values = pair_raw[:, head_dim:].astype(jnp.bfloat16)
    window_len = QW_DEV * seq_count
    window_rows = lax.dynamic_slice_in_dim(token_order, window_start[0], window_len)
    part_len = window_len // groups
    query_rows = lax.dynamic_slice_in_dim(window_rows, quarter * part_len, part_len)
    query_columns = jnp.take(gathered, query_rows, axis=2)
    query_raw = project_rows(
        query_columns, flat_weight[:, :head_dim], patch_weight, patch_bias, modulation
    )
    query_total, key_total = lax.psum(
        (jnp.sum(query_raw * query_raw, axis=1), jnp.sum(key_raw * key_raw, axis=1)), "seq"
    )
    norm_width = head_dim * seq_count
    queries = (
        query_raw * lax.rsqrt(query_total[:, None] / norm_width + norm_eps) * norm_gain[0]
    ).astype(jnp.bfloat16)
    key_rows = (
        key_raw * lax.rsqrt(key_total[:, None] / norm_width + norm_eps) * norm_gain[1]
    ).astype(jnp.bfloat16)
    queries = lax.all_gather(queries, ("grp", "tp"), axis=0, tiled=True)
    query_len = queries.shape[0]
    query_block = math.gcd(query_len, 512)
    score_scale = head_dim ** (-0.5)

    def attend(block_index):
        query_part = lax.dynamic_slice_in_dim(queries, block_index * query_block, query_block, 0)
        scores = (
            lax.dot_general(
                query_part, key_rows, (((1,), (1,)), ((), ())), preferred_element_type=jnp.float32
            )
            * score_scale
        )
        row_max = jnp.max(scores, axis=1)
        probs = jnp.exp(scores - row_max[:, None])
        row_sum = jnp.sum(probs, axis=1)
        row_acc = jnp.dot(probs.astype(jnp.bfloat16), values, preferred_element_type=jnp.float32)
        return (row_max, row_sum, row_acc)

    maxima, sums, accums = lax.map(attend, jnp.arange(query_len // query_block))
    maxima = maxima.reshape(query_len)
    sums = sums.reshape(query_len)
    accums = accums.reshape(query_len, head_dim)

    def combine(first, second):
        row_max = jnp.maximum(first[0], second[0])
        first_factor = jnp.exp(first[0] - row_max)
        second_factor = jnp.exp(second[0] - row_max)
        row_sum = first[1] * first_factor + second[1] * second_factor
        row_acc = first[2] * first_factor[:, None] + second[2] * second_factor[:, None]
        return (row_max, row_sum, row_acc)

    row_max, row_sum, row_acc = joined((maxima, sums, accums), ("grp", "tp"), combine)
    attention = (row_acc / row_sum[:, None]).astype(jnp.bfloat16)
    cols_dev = out_weight.shape[1]
    gate_cols = lax.dynamic_slice_in_dim(modulation[2], quarter * cols_dev, cols_dev)
    regrouped = lax.all_to_all(attention, "seq", split_axis=0, concat_axis=1, tiled=True)
    mixed_out = jnp.dot(
        regrouped,
        lax.all_gather(out_weight, "seq", axis=0, tiled=True),
        preferred_element_type=jnp.float32,
    )
    return (mixed_out * gate_cols).astype(jnp.bfloat16)


def solution(mesh):
    in_specs = (
        P("grp", None, "seq"),
        P(),
        P(),
        P(),
        P(None, None, "seq"),
        P(None, "seq"),
        P("seq", ("grp", "tp")),
        P(),
        P(),
    )
    out_specs = P("seq", ("grp", "tp"))
    return jax.shard_map(
        per_device, mesh=mesh, in_specs=in_specs, out_specs=out_specs, check_vma=False
    )
```

profile of v0, /device:TPU:0, one launch (start us, length us, event | category | flops | bytes accessed | tf_op | source)
XLA Modules:
  0.0 168.9 jit_solution(8679716140680726561)
XLA Ops:
  6.5 4.1 %collective-permute-start = (bf16[1,64,256]{2,1,0:T(8,128)(2,1)}, bf16[1,64,256]{2,1,0:T(8,128)(2,1)S(1)}, u32[]{:S(2)}, u32[]{:S(2)}) collective-permute-start(bf16[1,64,256]{2,1,0:T(8,128)(2,1)} %param.13), channel_id=1, source_target_pairs={{0,16},{16,0},{1,17},{17,1},{2,18},{18,2},{3,19},{19,3},{4,20},{20... | collective-permute-start | bytes 98312 | tf_op jit(solution)/shard_map/ppermute | solution.py:18
  11.3 1.7 %fusion.22 = (f32[1,5120]{1,0:T(1,128)}, f32[1,5120]{1,0:T(1,128)S(1)}, f32[1,5120]{1,0:T(1,128)S(1)}) fusion(f32[3,5120]{1,0:T(4,128)} %param.16), kind=kLoop, calls=%fused_computation.62 | loop fusion | flops 5120 | bytes 122880 | tf_op jit(solution)/shard_map/slice | solution.py:142
  13.0 1.3 slice_bitcast_fusion.1
  14.4 1.3 compare_and_fusion
  15.7 6.3 %copy.28 = bf16[5120,3,128]{0,2,1:T(8,128)(2,1)} copy(bf16[5120,3,128]{2,0,1:T(8,128)(2,1)} %param.17) | data formatting | bytes 7864320 | tf_op args[4]
  22.0 10.9 %all_gather.18 = bf16[2,64,2048]{2,1,0:T(8,128)(2,1)S(1)} all-gather(bf16[2,64,256]{2,1,0:T(8,128)(2,1)S(1)} %maximum_select_fusion), channel_id=1, replica_groups=mesh['grp'=2,'seq'=8,'tp'=2] {'seq'}, dimensions={2}, use_global_device_ids=true | all-gather | bytes 589824 | tf_op jit(solution)/shard_map/all_gather | solution.py:79
  33.0 0.7 copy.26
  33.7 1.6 fusion.9
  35.4 1.6 multiply_reduce_fusion
  37.0 0.5 copy-done.1
  37.5 2.5 %fusion.11 = f32[512,256]{0,1:T(8,128)S(1)} fusion(f32[512,5120,1]{1,0,2:T(8,128)S(1)} %get-tuple-element.357, f32[5120]{0:T(1024)S(1)} %bitcast.97, f32[5120]{0:T(1024)S(1)} %bitcast.95, f32[512]{0:T(512)S(1)} %add_rsqrt_fusion.1, f32[512]{0:T(512)S(1)} %broadcast_multiply_fusion, f32[5120]{0:T(1024)S(1)} %copy-done.3, bf16[5120,384]{0,1:T(8,128)(2,1)S(1)} %bitcast.83), kind=kOutput, calls=%fused_computation.26 | convolution fusion | flops 1357905920 | bytes 13697024 | tf_op jit(solution)/shard_map/while/body/eval_jaxpr/dot_general | solution.py:53
  40.1 1.6 gather_fusion
  41.7 1.2 fusion.19
  42.9 1.7 %fusion.23 = (f32[256]{0:T(256)S(1)}, f32[256,5120]{1,0:T(8,128)S(1)}) fusion(f32[5120]{0:T(1024)} %param.15, bf16[2,64,5120]{2,1,0:T(8,128)(2,1)S(1)} %bitcast.80, bf16[2,64,256]{1,0,2:T(2,128)(2,1)S(1)} %fusion.19), kind=kOutput, calls=%fused_computation.63 | convolution fusion | flops 338165504 | bytes 6640640 | tf_op jit(solution)/shard_map/while/body/eval_jaxpr/dot_general | solution.py:35
  44.6 0.7 multiply_reduce_fusion.1
  45.4 2.6 %multiply_reduce_fusion.3 = (f32[256]{0:T(256)S(1)}, f32[256,128]{0,1:T(8,128)S(1)}) fusion(bf16[5120,384]{0,1:T(8,128)(2,1)} %bitcast.82, f32[256,5120]{1,0:T(8,128)S(1)} %get-tuple-element.353, f32[5120]{0:T(1024)S(1)} %bitcast.98, f32[5120]{0:T(1024)S(1)} %bitcast.96, f32[256]{0:T(256)S(1)} %add_rsqrt_fusion.3, f32[256]{0:T(256)S(1)} %broadcast_multiply_fusion.1), kind=kOutput, calls=%fused_computation.42 | convolution fusion | flops 342163200 | bytes 6728704 | tf_op jit(solution)/shard_map/while/body/eval_jaxpr/dot_general | solution.py:53
  47.9 13.2 %all-reduce = (f32[256]{0:T(256)S(1)}, f32[512]{0:T(512)S(1)}) all-reduce(f32[256]{0:T(256)S(1)} %get-tuple-element.354, f32[512]{0:T(512)S(1)} %multiply_reduce_fusion.2), channel_id=1, replica_groups=mesh['grp'=2,'seq'=8,'tp'=2] {'seq'}, use_global_device_ids=true, to_apply=%region_3.4 | all-reduce | flops 768 | bytes 6144 | tf_op jit(solution)/shard_map/psum | solution.py:97
  61.1 0.1 multiply_convert_fusion
  61.2 0.1 copy.30
  61.4 0.1 multiply_convert_fusion.1
  61.5 14.4 %all_gather.19 = bf16[1024,128]{0,1:T(8,128)(2,1)S(1)} all-gather(bf16[256,128]{0,1:T(8,128)(2,1)S(1)} %multiply_convert_fusion.1), channel_id=1, replica_groups=mesh['grp'=2,'seq'=8,'tp'=2] {'grp','tp'}, dimensions={0}, use_global_device_ids=true | all-gather | bytes 327680 | tf_op jit(solution)/shard_map/all_gather | solution.py:107
  75.9 0.1 copy.31
  76.0 4.4 %while.11 = (s32[]{:T(128)}, f32[2,512]{1,0:T(2,128)S(1)}, f32[2,512]{1,0:T(2,128)S(1)}, f32[2,512,128]{2,1,0:T(8,128)S(1)}, s32[2]{0:T(128)S(1)}, /*index=5*/bf...) while((s32[]{:T(128)}, f32[2,512]{1,0:T(2,128)S(1)}, ...), condition=%wide.region_11.12_spmd, body=%wide.region_8.11_spmd.sunk | while | flops 135789568 | bytes 3817663 | solution.py:126
  76.0 0.6 dynamic_slice.81
  77.2 0.3 fusion.40
  77.5 0.4 fusion.42
  77.9 0.2 fusion.41
  78.2 0.6 dynamic_slice.81
  79.5 0.3 fusion.40
  79.8 0.4 fusion.42
  80.1 0.2 fusion.41
  80.4 0.8 copy-done.2
  81.3 0.7 all-gather.7.cloned.1.call-update
  82.0 13.5 %all-gather = f32[4,1,1024]{2,1,0:T(1,128)S(1)} all-gather(f32[1,1,1024]{2,1,0:T(1,128)S(1)} %reshape.73), channel_id=1, replica_groups=mesh['grp'=2,'seq'=8,'tp'=2] {'grp','tp'}, dimensions={0}, use_global_device_ids=true | all-gather | bytes 20480 | tf_op jit(solution)/shard_map/all_gather | solution.py:22
  95.6 13.8 %all-gather.1 = f32[4,1,1024]{2,1,0:T(1,128)S(1)} all-gather(f32[1,1,1024]{2,1,0:T(1,128)S(1)} %reshape.75), channel_id=1, replica_groups=mesh['grp'=2,'seq'=8,'tp'=2] {'grp','tp'}, dimensions={0}, use_global_device_ids=true | all-gather | bytes 20480 | tf_op jit(solution)/shard_map/all_gather | solution.py:22
  109.4 16.2 %all-gather.5.cloned.1.call-done = f32[4,1024,128]{2,1,0:T(8,128)} async-done(((f32[1,1024,128]{2,1,0:T(8,128)}), f32[4,1024,128]{2,1,0:T(8,128)}) %all-gather.5.cloned.1.call-update) | async-done | bytes 2097168 | tf_op jit(solution)/shard_map/all_gather | solution.py:22
  125.6 1.1 slice_bitcast_fusion
  126.7 4.7 %while.42 = (s32[]{:T(128)}, f32[1024]{0:T(1024)S(1)}, f32[1024]{0:T(1024)S(1)}, f32[1024,128]{1,0:T(8,128)S(1)}, f32[4,1024]{1,0:T(4,128)S(1)}, /*index=5*/f32[...) while((s32[]{:T(128)}, f32[1024]{0:T(1024)S(1)}, f32[1024]{0:T(1024)S(1)}, ...), condition=%wide.region_13.14_spmd, body=%wide.region_12.13_spmd.sunk | while | flops 399365 | bytes 1630359 | solution.py:28
  126.8 1.5 fusion.43
  128.3 1.5 fusion.43
  129.9 1.5 fusion.43
  131.4 0.9 divide_convert_fusion
  132.3 3.6 %all-to-all-start = ((bf16[8,128,128]{2,1,0:T(8,128)(2,1)}), bf16[8,128,128]{2,1,0:T(8,128)(2,1)S(1)}, u32[]{:S(2)}, u32[]{:S(2)}) async-start(bf16[8,128,128]{2,1,0:T(8,128)(2,1)} %bitcast.21), calls=%async_computation | async-start | bytes 524288 | tf_op jit(solution)/shard_map/all_to_all | solution.py:143
  135.9 0.7 dynamic-slice_reduce_fusion
  136.6 7.0 %all-to-all-done = bf16[8,128,128]{2,1,0:T(8,128)(2,1)S(1)} async-done(((bf16[8,128,128]{2,1,0:T(8,128)(2,1)}), bf16[8,128,128]{2,1,0:T(8,128)(2,1)S(1)}, u32[]{:S(2)}, u32[]{:S(2)}) %all-to-all-start) | async-done | bytes 262176 | tf_op jit(solution)/shard_map/all_to_all | solution.py:143
  143.6 0.2 copy.32
  143.8 15.3 %all-gather.7.cloned.1.call-done = bf16[1024,1280]{1,0:T(8,128)(2,1)} async-done(((bf16[128,1280]{1,0:T(8,128)(2,1)}), bf16[1024,1280]{1,0:T(8,128)(2,1)}) %all-gather.7.cloned.1.call-update) | async-done | bytes 2621456 | tf_op jit(solution)/shard_map/all_gather | solution.py:146
  159.1 3.0 %fusion.14 = bf16[128,1280]{1,0:T(8,128)(2,1)} fusion(bf16[128,1024]{0,1:T(8,128)(2,1)S(1)} %bitcast.84, bf16[1024,1280]{1,0:T(8,128)(2,1)} %all-gather.7.cloned.1.call-done, f32[1280]{0:T(1024)S(1)} %dynamic-slice_reduce_fusion), kind=kOutput, calls=%fused_computation.30 | convolution fusion | flops 335872000 | bytes 3216384 | tf_op jit(solution)/shard_map/dot_general | solution.py:144
  (54 shorter events, 0.5 us)
Async XLA Ops:
  6.5 27.2 %copy-start = (bf16[128,5120]{1,0:T(8,128)(2,1)S(1)}, bf16[128,5120]{1,0:T(8,128)(2,1)}, u32[]{:S(2)}) copy-start(bf16[128,5120]{1,0:T(8,128)(2,1)} %param.14) | copy-start | bytes 3932164
  6.5 15.5 %copy-start.4 = (bf16[1,64,256]{2,1,0:T(8,128)(2,1)S(1)}, bf16[1,64,256]{2,1,0:T(8,128)(2,1)}, u32[]{:S(2)}) copy-start(bf16[1,64,256]{2,1,0:T(8,128)(2,1)} %param.13) | copy-start | bytes 98308
  6.5 27.2 %copy-start.3 = (f32[5120]{0:T(1024)S(1)}, f32[5120]{0:T(1024)}, u32[]{:S(2)}) copy-start(f32[5120]{0:T(1024)} %param.15) | copy-start | bytes 61444
  6.5 119.1 %all-gather.5.cloned.1.call-start = ((), (), s32[]{:S(2)}) async-start(), calls=%async_computation.1 | async-start | bytes 2621440 | tf_op jit(solution)/shard_map/all_gather | solution.py:22
  6.5 15.5 %collective-permute-start = (bf16[1,64,256]{2,1,0:T(8,128)(2,1)}, bf16[1,64,256]{2,1,0:T(8,128)(2,1)S(1)}, u32[]{:S(2)}, u32[]{:S(2)}) collective-permute-start(bf16[1,64,256]{2,1,0:T(8,128)(2,1)} %param.13), channel_id=1, source_target_pairs={{0,16},{16,0},{1,17},{17,1},{2,18},{18,2},{3,19},{19,3},{4,20},{20... | collective-permute-start | bytes 98312 | tf_op jit(solution)/shard_map/ppermute | solution.py:18
  13.0 23.9 %copy-start.5 = (f32[1,5120]{1,0:T(1,128)}, f32[1,5120]{1,0:T(1,128)S(1)}, u32[]{:S(2)}) copy-start(f32[1,5120]{1,0:T(1,128)S(1)} %get-tuple-element.348) | copy-start | bytes 61444
  13.0 24.0 %copy-start.7 = (f32[1,5120]{1,0:T(1,128)}, f32[1,5120]{1,0:T(1,128)S(1)}, u32[]{:S(2)}) copy-start(f32[1,5120]{1,0:T(1,128)S(1)} %get-tuple-element.349) | copy-start | bytes 61444
  35.4 2.1 %copy-start.1 = (bf16[5120,3,128]{0,2,1:T(8,128)(2,1)S(1)}, bf16[5120,3,128]{0,2,1:T(8,128)(2,1)}, u32[]{:S(2)}) copy-start(bf16[5120,3,128]{0,2,1:T(8,128)(2,1)} %copy.28) | copy-start | bytes 11796484
  42.9 2.4 %copy-start.6 = (f32[1,5120]{1,0:T(1,128)S(1)}, f32[1,5120]{1,0:T(1,128)}, u32[]{:S(2)}) copy-start(f32[1,5120]{1,0:T(1,128)} %copy-done.5) | copy-start | bytes 61444
  42.9 2.4 %copy-start.8 = (f32[1,5120]{1,0:T(1,128)S(1)}, f32[1,5120]{1,0:T(1,128)}, u32[]{:S(2)}) copy-start(f32[1,5120]{1,0:T(1,128)} %copy-done.7) | copy-start | bytes 61444
  45.3 15.8 %copy-start.10 = (f32[128]{0:T(128)S(1)}, f32[128]{0:T(128)}, u32[]{:S(2)}) copy-start(f32[128]{0:T(128)} %get-tuple-element.350) | copy-start | bytes 1540
  45.3 16.0 %copy-start.9 = (f32[128]{0:T(128)S(1)}, f32[128]{0:T(128)}, u32[]{:S(2)}) copy-start(f32[128]{0:T(128)} %get-tuple-element.351) | copy-start | bytes 1540
  80.4 0.8 copy-start.2
  81.3 77.8 %all-gather.7.cloned.1.call-start = ((), (), s32[]{:S(2)}) async-start(), calls=%async_computation.2 | async-start | bytes 2949120 | tf_op jit(solution)/shard_map/all_gather | solution.py:146
  132.3 11.3 %all-to-all-start = ((bf16[8,128,128]{2,1,0:T(8,128)(2,1)}), bf16[8,128,128]{2,1,0:T(8,128)(2,1)S(1)}, u32[]{:S(2)}, u32[]{:S(2)}) async-start(bf16[8,128,128]{2,1,0:T(8,128)(2,1)} %bitcast.21), calls=%async_computation | async-start | bytes 524288 | tf_op jit(solution)/shard_map/all_to_all | solution.py:143
Sparse Core Ops, SparseCore 0:
  81.4 44.2 all-gather.4
  127.5 31.5 all-gather.6
where the time goes:
time: 170 us; the launch traced here: 169 us
  blocking collectives  65.9 us (39%)
  waiting for transfers between devices  39.2 us (23%)
  local copies, waits for them, and re-layouts  15 us (9%)
  between operations  14.3 us (8%)
  matrix products  12.8 us (8%)
  other arithmetic  12.6 us (7%)
  starting transfers between devices  7.78 us (5%)
    all_gather x2, blocking collectives, joined(): everything = jax.tree.map(lambda part: lax.all_gather(part, axis), array)  27.3 us
    all_gather x1, waiting for transfers between devices, joined(): everything = jax.tree.map(lambda part: lax.all_gather(part, axis), array)  16.2 us
    all_gather x1, waiting for transfers between devices, per_device(): lax.all_gather(out_weight, 'seq', axis=0, tiled=True)  15.3 us
    all_gather x1, blocking collectives, per_device(): queries = lax.all_gather(queries, ('grp', 'tp'), axis=0, tiled=True)  14.4 us
    psum x1, blocking collectives, per_device(): lax.psum((jnp.sum(query_raw * query_raw, axis=1), jnp.sum(key_raw * key_r...  13.2 us
    all_gather x1, blocking collectives, per_device(): gathered = lax.all_gather(paired, 'seq', axis=2, tiled=True)  10.9 us
    unnamed x27, local copies, waits for them, and re-layouts  7.73 us
    all_to_all x1, waiting for transfers between devices, per_device(): lax.all_to_all(attention, 'seq', split_axis=0, concat_axis=1, tiled=True)  6.96 us
  transfers between devices with their start and end apart: 4, of which 3 were waited for; matrix products, arithmetic and copies ran while one was open for 11% of the time, Pallas kernels for 0%

commit v1 on v0

--- a/solution.py
+++ b/solution.py
@@ -76,7 +76,12 @@
     paired = jnp.where(
         is_high, jnp.concatenate([latents, partner], 0), jnp.concatenate([partner, latents], 0)
     )
-    gathered = lax.all_gather(paired, "seq", axis=2, tiled=True)
+    ring = [paired]
+    for hop in range(7):
+        ring.append(lax.ppermute(ring[-1], "seq", [(dev, (dev + 1) % 8) for dev in range(8)]))
+    gathered = jnp.roll(
+        jnp.concatenate(ring[::-1], axis=2), (lax.axis_index("seq") + 1) * ring[0].shape[2], axis=2
+    )
     tokens = gathered.shape[2]
     key_count = tokens // groups
     flat_weight = qkv_weight.reshape(qkv_weight.shape[0], 3 * head_dim)

time: 170 us -> 188 us (1.11)
  waiting for transfers between devices: 39.2 us -> 68.6 us
  blocking collectives: 65.9 us -> 53.7 us
    ppermute x0 -> x7, waiting for transfers between devices: none -> 24.5 us  [per_device(): lax.ppermute(ring[-1], 'seq', [(dev, (dev + 1) % 8) for dev in range(8)])]
    all_gather x1 -> x0, blocking collectives: 10.9 us -> none  [per_device(): gathered = lax.all_gather(paired, 'seq', axis=2, tiled=True)]
    ppermute x1, waiting for transfers between devices: 0.01 us -> 2.48 us  [swapped(): return lax.ppermute(block, axis, route)]
    all_gather x1, waiting for transfers between devices: 16.2 us -> 18.7 us  [joined(): everything = jax.tree.map(lambda part: lax.all_gather(part, axis), array)]
    unnamed x27 -> x39, local copies, waits for them, and re-layouts: 7.73 us -> 7 us
  transfers between devices with their start and end apart: 4 -> 11, of which waited for: 3 -> 10; matrix products, arithmetic and copies ran while one was open for 11% -> 10% of each run, Pallas kernels for 0% -> 0%
where the time goes in v1:
time: 188 us; the launch traced here: 187 us
  waiting for transfers between devices  68.6 us (36%)
  blocking collectives  53.7 us (29%)
  between operations  14.5 us (8%)
  matrix products  14.2 us (8%)
  local copies, waits for them, and re-layouts  13.7 us (7%)
  other arithmetic  13.2 us (7%)
  starting transfers between devices  7.8 us (4%)
    all_gather x2, blocking collectives, joined(): everything = jax.tree.map(lambda part: lax.all_gather(part, axis), array)  27.5 us
    ppermute x7, waiting for transfers between devices, per_device(): lax.ppermute(ring[-1], 'seq', [(dev, (dev + 1) % 8) for dev in range(8)])  24.5 us
    all_gather x1, waiting for transfers between devices, joined(): everything = jax.tree.map(lambda part: lax.all_gather(part, axis), array)  18.7 us
    all_gather x1, waiting for transfers between devices, per_device(): lax.all_gather(out_weight, 'seq', axis=0, tiled=True)  15.3 us
    all_gather x1, blocking collectives, per_device(): queries = lax.all_gather(queries, ('grp', 'tp'), axis=0, tiled=True)  14.4 us
    psum x1, blocking collectives, per_device(): lax.psum((jnp.sum(query_raw * query_raw, axis=1), jnp.sum(key_raw * key_r...  11.8 us
    unnamed x39, local copies, waits for them, and re-layouts  7 us
    all_to_all x1, waiting for transfers between devices, per_device(): lax.all_to_all(attention, 'seq', split_axis=0, concat_axis=1, tiled=True)  6.99 us
  transfers between devices with their start and end apart: 11, of which 10 were waited for; matrix products, arithmetic and copies ran while one was open for 10% of the time, Pallas kernels for 0%

profile of v1, /device:TPU:0, one launch (start us, length us, event | category | flops | bytes accessed | tf_op | source)
XLA Modules:
  0.0 187.1 jit_solution(2520360465306774426)
XLA Ops:
  6.5 4.1 %collective-permute-start = (bf16[1,64,256]{2,1,0:T(8,128)(2,1)}, bf16[1,64,256]{2,1,0:T(8,128)(2,1)S(1)}, u32[]{:S(2)}, u32[]{:S(2)}) collective-permute-start(bf16[1,64,256]{2,1,0:T(8,128)(2,1)} %param.13), channel_id=1, source_target_pairs={{0,16},{16,0},{1,17},{17,1},{2,18},{18,2},{3,19},{19,3},{4,20},{20... | collective-permute-start | bytes 98312 | tf_op jit(solution)/shard_map/ppermute | solution.py:18
  10.6 2.5 %collective-permute-done = bf16[1,64,256]{2,1,0:T(8,128)(2,1)S(1)} collective-permute-done((bf16[1,64,256]{2,1,0:T(8,128)(2,1)}, bf16[1,64,256]{2,1,0:T(8,128)(2,1)S(1)}, u32[]{:S(2)}, u32[]{:S(2)}) %collective-permute-start) | collective-permute-done | bytes 32800 | tf_op jit(solution)/shard_map/ppermute | solution.py:18
  13.1 0.8 maximum_select_fusion
  14.0 4.6 %collective-permute-done.1 = bf16[2,64,256]{2,1,0:T(8,128)(2,1)S(1)} collective-permute-done((bf16[2,64,256]{2,1,0:T(8,128)(2,1)S(1)}, bf16[2,64,256]{2,1,0:T(8,128)(2,1)S(1)}, u32[]{:S(2)}, u32[]{:S(2)}) %collective-permute-start.1) | collective-permute-done | bytes 65568 | tf_op jit(solution)/shard_map/ppermute | solution.py:81
  18.6 4.6 %collective-permute-done.2 = bf16[2,64,256]{2,1,0:T(8,128)(2,1)S(1)} collective-permute-done((bf16[2,64,256]{2,1,0:T(8,128)(2,1)S(1)}, bf16[2,64,256]{2,1,0:T(8,128)(2,1)S(1)}, u32[]{:S(2)}, u32[]{:S(2)}) %collective-permute-start.2) | collective-permute-done | bytes 65568 | tf_op jit(solution)/shard_map/ppermute | solution.py:81
  23.2 4.6 %collective-permute-done.3 = bf16[2,64,256]{2,1,0:T(8,128)(2,1)S(1)} collective-permute-done((bf16[2,64,256]{2,1,0:T(8,128)(2,1)S(1)}, bf16[2,64,256]{2,1,0:T(8,128)(2,1)S(1)}, u32[]{:S(2)}, u32[]{:S(2)}) %collective-permute-start.3) | collective-permute-done | bytes 65568 | tf_op jit(solution)/shard_map/ppermute | solution.py:81
  27.8 1.7 fusion.22
  29.5 2.9 %collective-permute-done.4 = bf16[2,64,256]{2,1,0:T(8,128)(2,1)S(1)} collective-permute-done((bf16[2,64,256]{2,1,0:T(8,128)(2,1)S(1)}, bf16[2,64,256]{2,1,0:T(8,128)(2,1)S(1)}, u32[]{:S(2)}, u32[]{:S(2)}) %collective-permute-start.4) | collective-permute-done | bytes 65568 | tf_op jit(solution)/shard_map/ppermute | solution.py:81
  32.4 1.3 slice_bitcast_fusion.1
  33.7 6.3 %copy.28 = bf16[5120,3,128]{0,2,1:T(8,128)(2,1)} copy(bf16[5120,3,128]{2,0,1:T(8,128)(2,1)} %param.17) | data formatting | bytes 7864320 | tf_op args[4]
  40.8 1.3 compare_and_fusion
  42.1 3.3 %collective-permute-done.6 = bf16[2,64,256]{2,1,0:T(8,128)(2,1)S(1)} collective-permute-done((bf16[2,64,256]{2,1,0:T(8,128)(2,1)S(1)}, bf16[2,64,256]{2,1,0:T(8,128)(2,1)S(1)}, u32[]{:S(2)}, u32[]{:S(2)}) %collective-permute-start.6) | collective-permute-done | bytes 65568 | tf_op jit(solution)/shard_map/ppermute | solution.py:81
  45.4 4.6 %collective-permute-done.7 = bf16[2,64,256]{2,1,0:T(8,128)(2,1)S(1)} collective-permute-done((bf16[2,64,256]{2,1,0:T(8,128)(2,1)S(1)}, bf16[2,64,256]{2,1,0:T(8,128)(2,1)S(1)}, u32[]{:S(2)}, u32[]{:S(2)}) %collective-permute-start.7) | collective-permute-done | bytes 65568 | tf_op jit(solution)/shard_map/ppermute | solution.py:81
  50.3 1.7 fusion.9
  52.0 1.6 multiply_reduce_fusion
  53.6 0.5 copy-done.1
  54.1 2.5 %fusion.11 = f32[512,256]{0,1:T(8,128)S(1)} fusion(f32[512,5120,1]{1,0,2:T(8,128)S(1)} %get-tuple-element.357, f32[5120]{0:T(1024)S(1)} %bitcast.97, f32[5120]{0:T(1024)S(1)} %bitcast.95, f32[512]{0:T(512)S(1)} %add_rsqrt_fusion.1, f32[512]{0:T(512)S(1)} %broadcast_multiply_fusion, f32[5120]{0:T(1024)S(1)} %copy-done.2, bf16[5120,384]{0,1:T(8,128)(2,1)S(1)} %bitcast.83), kind=kOutput, calls=%fused_computation.26 | convolution fusion | flops 1357905920 | bytes 13697024 | tf_op jit(solution)/shard_map/while/body/eval_jaxpr/dot_general | solution.py:53
  56.7 0.8 copy.26
  57.5 0.9 gather_fusion
  58.4 1.0 fusion.19
  59.4 1.7 fusion.23
  61.1 0.7 multiply_reduce_fusion.1
  61.8 2.6 %multiply_reduce_fusion.3 = (f32[256]{0:T(256)S(1)}, f32[256,128]{0,1:T(8,128)S(1)}) fusion(bf16[5120,384]{0,1:T(8,128)(2,1)} %bitcast.82, f32[256,5120]{1,0:T(8,128)S(1)} %get-tuple-element.353, f32[5120]{0:T(1024)S(1)} %bitcast.98, f32[5120]{0:T(1024)S(1)} %bitcast.96, f32[256]{0:T(256)S(1)} %add_rsqrt_fusion.3, f32[256]{0:T(256)S(1)} %broadcast_multiply_fusion.1), kind=kOutput, calls=%fused_computation.42 | convolution fusion | flops 342163200 | bytes 6728704 | tf_op jit(solution)/shard_map/while/body/eval_jaxpr/dot_general | solution.py:53
  64.4 11.8 %all-reduce = (f32[256]{0:T(256)S(1)}, f32[512]{0:T(512)S(1)}) all-reduce(f32[256]{0:T(256)S(1)} %get-tuple-element.354, f32[512]{0:T(512)S(1)} %multiply_reduce_fusion.2), channel_id=1, replica_groups=mesh['grp'=2,'seq'=8,'tp'=2] {'seq'}, use_global_device_ids=true, to_apply=%region_3.4 | all-reduce | flops 768 | bytes 6144 | tf_op jit(solution)/shard_map/psum | solution.py:102
  76.5 14.4 %all_gather.15 = bf16[1024,128]{0,1:T(8,128)(2,1)S(1)} all-gather(bf16[256,128]{0,1:T(8,128)(2,1)S(1)} %multiply_convert_fusion.1), channel_id=1, replica_groups=mesh['grp'=2,'seq'=8,'tp'=2] {'grp','tp'}, dimensions={0}, use_global_device_ids=true | all-gather | bytes 327680 | tf_op jit(solution)/shard_map/all_gather | solution.py:112
  91.1 5.8 %while.11 = (s32[]{:T(128)}, f32[2,512]{1,0:T(2,128)S(1)}, f32[2,512]{1,0:T(2,128)S(1)}, f32[2,512,128]{2,1,0:T(8,128)}, s32[2]{0:T(128)S(1)}, /*index=5*/bf16[1...) while((s32[]{:T(128)}, f32[2,512]{1,0:T(2,128)S(1)}, ...), condition=%wide.region_11.12_spmd, body=%wide.region_8.11_spmd.sunk | while | flops 135789568 | bytes 3818171 | solution.py:131
  91.1 0.6 dynamic_slice.91
  92.3 0.3 fusion.40
  92.6 1.1 fusion.42
  93.7 0.2 fusion.41
  94.0 0.6 dynamic_slice.91
  95.2 0.3 fusion.40
  95.5 1.0 fusion.42
  96.9 0.7 all-gather.7.cloned.1.call-update
  97.6 13.6 %all-gather = f32[4,1,1024]{2,1,0:T(1,128)S(1)} all-gather(f32[1,1,1024]{2,1,0:T(1,128)S(1)} %reshape.73), channel_id=1, replica_groups=mesh['grp'=2,'seq'=8,'tp'=2] {'grp','tp'}, dimensions={0}, use_global_device_ids=true | all-gather | bytes 20480 | tf_op jit(solution)/shard_map/all_gather | solution.py:22
  111.2 13.9 %all-gather.1 = f32[4,1,1024]{2,1,0:T(1,128)S(1)} all-gather(f32[1,1,1024]{2,1,0:T(1,128)S(1)} %reshape.75), channel_id=1, replica_groups=mesh['grp'=2,'seq'=8,'tp'=2] {'grp','tp'}, dimensions={0}, use_global_device_ids=true | all-gather | bytes 20480 | tf_op jit(solution)/shard_map/all_gather | solution.py:22
  125.1 18.7 %all-gather.5.cloned.1.call-done = f32[4,1024,128]{2,1,0:T(8,128)} async-done(((f32[1,1024,128]{2,1,0:T(8,128)}), f32[4,1024,128]{2,1,0:T(8,128)}) %all-gather.5.cloned.1.call-update) | async-done | bytes 2097168 | tf_op jit(solution)/shard_map/all_gather | solution.py:22
  143.8 1.1 slice_bitcast_fusion
  144.9 4.7 %while.42 = (s32[]{:T(128)}, f32[1024]{0:T(1024)S(1)}, f32[1024]{0:T(1024)S(1)}, f32[1024,128]{1,0:T(8,128)S(1)}, f32[4,1024]{1,0:T(4,128)S(1)}, /*index=5*/f32[...) while((s32[]{:T(128)}, f32[1024]{0:T(1024)S(1)}, f32[1024]{0:T(1024)S(1)}, ...), condition=%wide.region_13.14_spmd, body=%wide.region_12.13_spmd.sunk | while | flops 399365 | bytes 1630359 | solution.py:28
  144.9 1.5 fusion.43
  146.5 1.5 fusion.43
  148.1 1.5 fusion.43
  149.6 0.9 divide_convert_fusion
  150.5 3.6 %all-to-all-start = ((bf16[8,128,128]{2,1,0:T(8,128)(2,1)}), bf16[8,128,128]{2,1,0:T(8,128)(2,1)S(1)}, u32[]{:S(2)}, u32[]{:S(2)}) async-start(bf16[8,128,128]{2,1,0:T(8,128)(2,1)} %bitcast.21), calls=%async_computation | async-start | bytes 524288 | tf_op jit(solution)/shard_map/all_to_all | solution.py:148
  154.0 0.7 dynamic-slice_reduce_fusion
  154.8 7.0 %all-to-all-done = bf16[8,128,128]{2,1,0:T(8,128)(2,1)S(1)} async-done(((bf16[8,128,128]{2,1,0:T(8,128)(2,1)}), bf16[8,128,128]{2,1,0:T(8,128)(2,1)S(1)}, u32[]{:S(2)}, u32[]{:S(2)}) %all-to-all-start) | async-done | bytes 262176 | tf_op jit(solution)/shard_map/all_to_all | solution.py:148
  161.9 15.3 %all-gather.7.cloned.1.call-done = bf16[1024,1280]{1,0:T(8,128)(2,1)} async-done(((bf16[128,1280]{1,0:T(8,128)(2,1)}), bf16[1024,1280]{1,0:T(8,128)(2,1)}) %all-gather.7.cloned.1.call-update) | async-done | bytes 2621456 | tf_op jit(solution)/shard_map/all_gather | solution.py:151
  177.2 3.0 %fusion.14 = bf16[128,1280]{1,0:T(8,128)(2,1)} fusion(bf16[128,1024]{0,1:T(8,128)(2,1)S(1)} %bitcast.84, bf16[1024,1280]{1,0:T(8,128)(2,1)} %all-gather.7.cloned.1.call-done, f32[1280]{0:T(1024)S(1)} %dynamic-slice_reduce_fusion), kind=kOutput, calls=%fused_computation.30 | convolution fusion | flops 335872000 | bytes 3216384 | tf_op jit(solution)/shard_map/dot_general | solution.py:149
  (82 shorter events, 1.6 us)
Async XLA Ops:
  6.5 43.7 %copy-start = (bf16[128,5120]{1,0:T(8,128)(2,1)S(1)}, bf16[128,5120]{1,0:T(8,128)(2,1)}, u32[]{:S(2)}) copy-start(bf16[128,5120]{1,0:T(8,128)(2,1)} %param.14) | copy-start | bytes 3932164
  6.5 43.5 %copy-start.3 = (bf16[1,64,256]{2,1,0:T(8,128)(2,1)S(1)}, bf16[1,64,256]{2,1,0:T(8,128)(2,1)}, u32[]{:S(2)}) copy-start(bf16[1,64,256]{2,1,0:T(8,128)(2,1)} %param.13) | copy-start | bytes 98308
  6.5 137.3 %all-gather.5.cloned.1.call-start = ((), (), s32[]{:S(2)}) async-start(), calls=%async_computation.1 | async-start | bytes 2621440 | tf_op jit(solution)/shard_map/all_gather | solution.py:22
  6.5 6.5 %collective-permute-start = (bf16[1,64,256]{2,1,0:T(8,128)(2,1)}, bf16[1,64,256]{2,1,0:T(8,128)(2,1)S(1)}, u32[]{:S(2)}, u32[]{:S(2)}) collective-permute-start(bf16[1,64,256]{2,1,0:T(8,128)(2,1)} %param.13), channel_id=1, source_target_pairs={{0,16},{16,0},{1,17},{17,1},{2,18},{18,2},{3,19},{19,3},{4,20},{20... | collective-permute-start | bytes 98312 | tf_op jit(solution)/shard_map/ppermute | solution.py:18
  13.9 4.6 %collective-permute-start.1 = (bf16[2,64,256]{2,1,0:T(8,128)(2,1)S(1)}, bf16[2,64,256]{2,1,0:T(8,128)(2,1)S(1)}, u32[]{:S(2)}, u32[]{:S(2)}) collective-permute-start(bf16[2,64,256]{2,1,0:T(8,128)(2,1)S(1)} %maximum_select_fusion), channel_id=1, source_target_pairs={{0,2},{2,4},{4,6},{6,8},{8,10},{10,12},{12,14},{14,0},{1,3},{3,5},... | collective-permute-start | bytes 196616 | tf_op jit(solution)/shard_map/ppermute | solution.py:81
  18.6 4.6 %collective-permute-start.2 = (bf16[2,64,256]{2,1,0:T(8,128)(2,1)S(1)}, bf16[2,64,256]{2,1,0:T(8,128)(2,1)S(1)}, u32[]{:S(2)}, u32[]{:S(2)}) collective-permute-start(bf16[2,64,256]{2,1,0:T(8,128)(2,1)S(1)} %collective-permute-done.1), channel_id=1, source_target_pairs={{0,2},{2,4},{4,6},{6,8},{8,10},{10,12},{12,14},{14,0},{1,3},{3,5},... | collective-permute-start | bytes 196616 | tf_op jit(solution)/shard_map/ppermute | solution.py:81
  23.2 4.6 %collective-permute-start.3 = (bf16[2,64,256]{2,1,0:T(8,128)(2,1)S(1)}, bf16[2,64,256]{2,1,0:T(8,128)(2,1)S(1)}, u32[]{:S(2)}, u32[]{:S(2)}) collective-permute-start(bf16[2,64,256]{2,1,0:T(8,128)(2,1)S(1)} %collective-permute-done.2), channel_id=1, source_target_pairs={{0,2},{2,4},{4,6},{6,8},{8,10},{10,12},{12,14},{14,0},{1,3},{3,5},... | collective-permute-start | bytes 196616 | tf_op jit(solution)/shard_map/ppermute | solution.py:81
  27.8 4.6 %collective-permute-start.4 = (bf16[2,64,256]{2,1,0:T(8,128)(2,1)S(1)}, bf16[2,64,256]{2,1,0:T(8,128)(2,1)S(1)}, u32[]{:S(2)}, u32[]{:S(2)}) collective-permute-start(bf16[2,64,256]{2,1,0:T(8,128)(2,1)S(1)} %collective-permute-done.3), channel_id=1, source_target_pairs={{0,2},{2,4},{4,6},{6,8},{8,10},{10,12},{12,14},{14,0},{1,3},{3,5},... | collective-permute-start | bytes 196616 | tf_op jit(solution)/shard_map/ppermute | solution.py:81
  29.5 24.1 %copy-start.4 = (f32[1,5120]{1,0:T(1,128)}, f32[1,5120]{1,0:T(1,128)S(1)}, u32[]{:S(2)}) copy-start(f32[1,5120]{1,0:T(1,128)S(1)} %get-tuple-element.348) | copy-start | bytes 61444
  29.5 24.1 %copy-start.6 = (f32[1,5120]{1,0:T(1,128)}, f32[1,5120]{1,0:T(1,128)S(1)}, u32[]{:S(2)}) copy-start(f32[1,5120]{1,0:T(1,128)S(1)} %get-tuple-element.349) | copy-start | bytes 61444
  32.4 8.4 %collective-permute-start.5 = (bf16[2,64,256]{2,1,0:T(8,128)(2,1)S(1)}, bf16[2,64,256]{2,1,0:T(8,128)(2,1)S(1)}, u32[]{:S(2)}, u32[]{:S(2)}) collective-permute-start(bf16[2,64,256]{2,1,0:T(8,128)(2,1)S(1)} %collective-permute-done.4), channel_id=1, source_target_pairs={{0,2},{2,4},{4,6},{6,8},{8,10},{10,12},{12,14},{14,0},{1,3},{3,5},... | collective-permute-start | bytes 196616 | tf_op jit(solution)/shard_map/ppermute | solution.py:81
  33.7 16.6 %copy-start.2 = (f32[5120]{0:T(1024)S(1)}, f32[5120]{0:T(1024)}, u32[]{:S(2)}) copy-start(f32[5120]{0:T(1024)} %param.15) | copy-start | bytes 61444
  40.7 4.6 %collective-permute-start.6 = (bf16[2,64,256]{2,1,0:T(8,128)(2,1)S(1)}, bf16[2,64,256]{2,1,0:T(8,128)(2,1)S(1)}, u32[]{:S(2)}, u32[]{:S(2)}) collective-permute-start(bf16[2,64,256]{2,1,0:T(8,128)(2,1)S(1)} %collective-permute-done.5), channel_id=1, source_target_pairs={{0,2},{2,4},{4,6},{6,8},{8,10},{10,12},{12,14},{14,0},{1,3},{3,5},... | collective-permute-start | bytes 196616 | tf_op jit(solution)/shard_map/ppermute | solution.py:81
  45.4 4.6 %collective-permute-start.7 = (bf16[2,64,256]{2,1,0:T(8,128)(2,1)S(1)}, bf16[2,64,256]{2,1,0:T(8,128)(2,1)S(1)}, u32[]{:S(2)}, u32[]{:S(2)}) collective-permute-start(bf16[2,64,256]{2,1,0:T(8,128)(2,1)S(1)} %collective-permute-done.6), channel_id=1, source_target_pairs={{0,2},{2,4},{4,6},{6,8},{8,10},{10,12},{12,14},{14,0},{1,3},{3,5},... | collective-permute-start | bytes 196616 | tf_op jit(solution)/shard_map/ppermute | solution.py:81
  52.0 2.1 %copy-start.1 = (bf16[5120,3,128]{0,2,1:T(8,128)(2,1)S(1)}, bf16[5120,3,128]{0,2,1:T(8,128)(2,1)}, u32[]{:S(2)}) copy-start(bf16[5120,3,128]{0,2,1:T(8,128)(2,1)} %copy.28) | copy-start | bytes 11796484
  59.4 2.4 %copy-start.5 = (f32[1,5120]{1,0:T(1,128)S(1)}, f32[1,5120]{1,0:T(1,128)}, u32[]{:S(2)}) copy-start(f32[1,5120]{1,0:T(1,128)} %copy-done.4) | copy-start | bytes 61444
  59.4 2.4 %copy-start.7 = (f32[1,5120]{1,0:T(1,128)S(1)}, f32[1,5120]{1,0:T(1,128)}, u32[]{:S(2)}) copy-start(f32[1,5120]{1,0:T(1,128)} %copy-done.6) | copy-start | bytes 61444
  61.8 14.4 %copy-start.9 = (f32[128]{0:T(128)S(1)}, f32[128]{0:T(128)}, u32[]{:S(2)}) copy-start(f32[128]{0:T(128)} %get-tuple-element.350) | copy-start | bytes 1540
  61.8 14.6 %copy-start.8 = (f32[128]{0:T(128)S(1)}, f32[128]{0:T(128)}, u32[]{:S(2)}) copy-start(f32[128]{0:T(128)} %get-tuple-element.351) | copy-start | bytes 1540
  96.9 80.4 %all-gather.7.cloned.1.call-start = ((), (), s32[]{:S(2)}) async-start(), calls=%async_computation.2 | async-start | bytes 2949120 | tf_op jit(solution)/shard_map/all_gather | solution.py:151
  150.5 11.3 %all-to-all-start = ((bf16[8,128,128]{2,1,0:T(8,128)(2,1)}), bf16[8,128,128]{2,1,0:T(8,128)(2,1)S(1)}, u32[]{:S(2)}, u32[]{:S(2)}) async-start(bf16[8,128,128]{2,1,0:T(8,128)(2,1)} %bitcast.21), calls=%async_computation | async-start | bytes 524288 | tf_op jit(solution)/shard_map/all_to_all | solution.py:148
Sparse Core Ops, SparseCore 0:
  97.0 46.7 all-gather.4
  145.7 31.4 all-gather.6
